TPU v7x, 256 devices: a whole 4x4x8 slice. The times are simulated.
256 devices in a mesh: ctx: 64 (over x, z, core), head: 4 (over y).
Axes of the slice: x: 4, y: 4, z: 8, core: 2. Of those that a mesh axis runs over, the one named last changes fastest.
Arguments:
- queries: bfloat16 [512, 5120], P(None, 'head'), may hold values from -18 to 18
- keys: bfloat16 [32768, 1024], P('ctx', 'head'), may hold values from -20 to 20
- values: bfloat16 [32768, 1024], P('ctx', 'head'), may hold values from -6 to 6
- stretch_lengths: int32 [256], replicated, may hold values from 1 to 512, 32768 in all
- query_pos: int32 [512], replicated, may hold values from 0 to 511, each once
Outputs:
- attended: bfloat16 [512, 5120], P('ctx', 'head')
- stretch_mass: float32 [256, 512], replicated
Inputs may be any that keep to these rules, and one draw needn't show every extreme that they name: `stretch_lengths`: stretch lengths sum to 32768; the longest is exactly 512. `query_pos`: each of 0 to 511 appears once.
All inputs are finite; a program needn't handle non-finite values.
Results may differ from a plain program's by a relative error of at most 0.0076.
Values sent between devices are 32-bit elements; how exact they have to be, the bound alone decides.
A program may use at most 64 MiB of HBM per device.

v0:
```python
import jax
import jax.numpy as jnp
from jax import lax
from jax.sharding import PartitionSpec as P

HD = 128


ROPE_BASE = 1000000.0


def rope_queries(queries, query_pos):
    query_count = queries.shape[0]
    head_count = queries.shape[1] // HD
    half_dim = HD // 2
    frequency = ROPE_BASE ** (-(jnp.arange(half_dim, dtype=jnp.float32) * 2.0 / HD))
    angles = query_pos.astype(jnp.float32)[:, None] * frequency[None, :]
    cosine = jnp.cos(angles)[:, None, :]
    sin_part = jnp.sin(angles)[:, None, :]
    as_float = queries.astype(jnp.float32).reshape(query_count, head_count, HD)
    front_half = as_float[..., :half_dim]
    back_half = as_float[..., half_dim:]
    rotated = jnp.concatenate(
        [front_half * cosine - back_half * sin_part, back_half * cosine + front_half * sin_part],
        axis=-1,
    )
    return rotated.astype(jnp.bfloat16)


def local(queries, keys, values, stretch_lengths, query_pos):
    roped = rope_queries(queries, query_pos)
    query_count = roped.shape[0]
    heads_here = roped.shape[1]
    kv_here = keys.shape[1] // HD
    group_size = heads_here // kv_here
    tok_here = keys.shape[0]
    stretch_count = stretch_lengths.shape[0]
    block_rows = min(64, query_count)
    block_count = query_count // block_rows
    q_blocks = roped.reshape(block_count, block_rows, kv_here, group_size, HD)
    key_rows = keys.reshape(tok_here, kv_here, HD)
    value_rows = values.reshape(tok_here, kv_here, HD)
    starts = jnp.cumsum(stretch_lengths) - stretch_lengths
    stretch_ends = starts + stretch_lengths
    key_position = lax.axis_index("ctx") * tok_here + jnp.arange(tok_here, dtype=jnp.int32)
    onehot = (
        (key_position[:, None] >= starts[None, :]) & (key_position[:, None] < stretch_ends[None, :])
    ).astype(jnp.bfloat16)
    score_scale = HD ** (-0.5)

    def score_block(q_block):
        return (
            jnp.einsum("qgjd,kgd->gjqk", q_block, key_rows, preferred_element_type=jnp.float32)
            * score_scale
        )

    def weigh(logits, row_top):
        weights = jnp.exp(logits - row_top[..., None])
        row_sum = jnp.sum(weights, axis=-1)
        rounded = weights.astype(jnp.bfloat16)
        weighted = jnp.einsum(
            "gjqk,kgd->gjqd", rounded, value_rows, preferred_element_type=jnp.float32
        )
        return (row_sum, weighted)

    local_top = lax.map(lambda q_block: score_block(q_block).max(-1), q_blocks)
    row_top = lax.pmax(local_top, "ctx")
    row_sum, weighted = lax.map(
        lambda pieces: weigh(score_block(pieces[0]), pieces[1]), (q_blocks, row_top)
    )
    whole_sum = lax.psum(row_sum, "ctx")
    inverse = 1.0 / whole_sum

    def mass_block(pieces):
        q_block, top_block, inverse_block = pieces
        logits = score_block(q_block)
        rounded = jnp.exp(logits - top_block[..., None]).astype(jnp.bfloat16)
        share = jnp.sum(rounded.astype(jnp.float32) * inverse_block[..., None], axis=(0, 1))
        high_part = share.astype(jnp.bfloat16)
        low_part = (share - high_part.astype(jnp.float32)).astype(jnp.bfloat16)
        return jnp.einsum(
            "qk,kc->cq", high_part, onehot, preferred_element_type=jnp.float32
        ) + jnp.einsum("qk,kc->cq", low_part, onehot, preferred_element_type=jnp.float32)

    block_mass = lax.map(mass_block, (q_blocks, row_top, inverse))
    mass_factor = stretch_count / (heads_here * lax.axis_size("head"))
    mass_term = block_mass.transpose(1, 0, 2).reshape(stretch_count, query_count) * mass_factor
    stretch_mass = lax.psum(mass_term, ("ctx", "head"))
    scaled = weighted.transpose(0, 3, 1, 2, 4).reshape(query_count, heads_here * HD)
    inverse_rows = inverse.transpose(0, 3, 1, 2).reshape(query_count, heads_here)
    rows_here = query_count // lax.axis_size("ctx")
    inverse_here = lax.dynamic_slice_in_dim(
        inverse_rows, lax.axis_index("ctx") * rows_here, rows_here, 0
    )
    whole_out = lax.psum(scaled, "ctx")
    summed = lax.dynamic_slice_in_dim(whole_out, lax.axis_index("ctx") * rows_here, rows_here, 0)
    normalized = summed.reshape(rows_here, heads_here, HD) * inverse_here[..., None]
    attended = normalized.reshape(rows_here, heads_here * HD).astype(jnp.bfloat16)
    return (attended, stretch_mass)


def solution(mesh):
    placed = (P(None, "head"), P("ctx", "head"), P("ctx", "head"), P(), P())
    return jax.shard_map(
        local, mesh=mesh, in_specs=placed, out_specs=(P("ctx", "head"), P()), check_vma=False
    )
```

profile of v0, /device:TPU:1, one launch (start us, length us, event | category | flops | bytes accessed | tf_op | source)
XLA Modules:
  0.0 1026.2 jit_solution(5724059091392489724)
XLA Ops:
  15.3 1.8 concatenate.9
  17.0 1.8 concatenate.10
  18.8 2.2 pad_maximum_fusion
  21.0 3.3 copy.14
  24.3 11.8 %while.33 = (s32[]{:T(128)}, f32[8,2,5,64]{3,2,1,0:T(8,128)S(1)}, bf16[8,64,2,5,128]{4,1,3,2,0:T(8,128)(2,1)}, bf16[512,2,128]{2,0,1:T(8,128)(2,1)}, s32[]{:T(128)}) while((s32[]{:T(128)}, f32[8,2,5,64]{3,2,1,0:T(8,128)S(1)}, bf16[8,64,2,5,128]{4,1,3,2,0:T(8,128)(2,1)}, bf16[512,2,128]{2,0,1:T(8,128)(2,1)}, s32[]{:T(128)}) %tuple.66), condition=%wide.region_2.3_spmd, body=%wide.region_0.2_spmd.sunk | while | flops 84540800 | bytes 445005 | solution.py:66
  28.7 1.4 fusion.59
  36.1 249.4 %pmax.7 = f32[8,2,5,64]{3,2,1,0:T(8,128)S(1)} all-reduce(f32[8,2,5,64]{3,2,1,0:T(8,128)S(1)} %get-tuple-element.99), channel_id=1, replica_groups=mesh['ctx'=64,'head'=4] {'ctx'}, use_global_device_ids=true, to_apply=%region_3.4 | all-reduce | flops 5120 | bytes 40960 | tf_op jit(solution)/shard_map/pmax | solution.py:67
  285.6 20.9 %while.34 = (s32[]{:T(128)}, f32[8,2,5,64]{3,2,1,0:T(8,128)S(1)}, f32[8,2,5,64,128]{4,3,2,1,0:T(8,128)}, bf16[8,64,2,5,128]{4,1,3,2,0:T(8,128)(2,1)}, bf16[512,2...) while((s32[]{:T(128)}, f32[8,2,5,64]{3,2,1,0:T(8,128)S(1)}, ...), condition=%wide.region_6.7_spmd, body=%wide.region_4.6_spmd.sunk | while | flops 169082240 | bytes 2353261 | solution.py:68
  285.6 1.5 fusion.62
  288.2 1.5 fusion.62
  290.8 1.5 fusion.62
  293.4 1.5 fusion.62
  296.0 1.5 fusion.62
  298.6 1.5 fusion.62
  301.2 1.5 fusion.62
  303.8 1.5 fusion.62
  306.4 246.1 %psum.22 = f32[8,2,5,64]{3,2,1,0:T(8,128)S(1)} all-reduce(f32[8,2,5,64]{3,2,1,0:T(8,128)S(1)} %get-tuple-element.101), channel_id=1, replica_groups=mesh['ctx'=64,'head'=4] {'ctx'}, use_global_device_ids=true, to_apply=%region_8.9 | all-reduce | flops 5120 | bytes 40960 | tf_op jit(solution)/shard_map/psum | solution.py:71
  552.6 16.8 %while.35 = (s32[]{:T(128)}, f32[8,256,64]{1,2,0:T(8,128)S(1)}, bf16[8,64,2,5,128]{4,1,3,2,0:T(8,128)(2,1)}, bf16[512,2,128]{2,0,1:T(8,128)(2,1)}, f32[8,2,5,64]...) while((s32[]{:T(128)}, f32[8,256,64]{1,2,0:T(8,128)S(1)}, ...), condition=%wide.region_13.14_spmd.clone, body=%wide.region_11.13_spmd.clone.sunk | while | flops 120602624 | bytes 1039481 | solution.py:85
  552.6 1.6 fusion.67
  554.8 1.5 fusion.67
  556.9 1.5 fusion.67
  559.0 1.5 fusion.67
  561.1 1.5 fusion.67
  563.1 1.5 fusion.67
  565.2 1.5 fusion.67
  567.3 1.5 fusion.67
  570.3 3.5 copy.17
  573.7 4.7 reshape.126
  578.7 244.6 %all-reduce.5.cloned.1.call-done = f32[256,512]{0,1:T(8,128)} async-done(((f32[256,512]{0,1:T(8,128)}), f32[256,512]{0,1:T(8,128)}) %all-reduce.5.cloned.1.call-update) | async-done | bytes 524304 | tf_op jit(solution)/shard_map/psum | solution.py:88
  823.3 2.0 copy.21
  825.3 192.7 %all-reduce.3.cloned.1.call-done = f32[512,1280]{1,0:T(8,128)} async-done(((f32[512,1280]{1,0:T(8,128)}), f32[512,1280]{1,0:T(8,128)}) %all-reduce.3.cloned.1.call-update) | async-done | bytes 2621456 | tf_op jit(solution)/shard_map/psum | solution.py:95
  1017.9 1.5 fusion.39
  (96 shorter events, 32.3 us)
Async XLA Ops:
  7.2 6.0 copy-start.1
  7.2 816.1 %all-reduce.5.cloned.1.call-start = ((), (), s32[]{:S(2)}) async-start(), calls=%async_computation.1 | async-start | bytes 1048576 | tf_op jit(solution)/shard_map/psum | solution.py:88
  552.6 17.7 %copy-start = (f32[8,2,5,64,128]{4,3,2,1,0:T(8,128)S(1)}, f32[8,2,5,64,128]{4,3,2,1,0:T(8,128)}, u32[]{:S(2)}) copy-start(f32[8,2,5,64,128]{4,3,2,1,0:T(8,128)} %get-tuple-element.100) | copy-start | bytes 7864324
  570.2 447.7 %all-reduce.3.cloned.1.call-start = ((), (), s32[]{:S(2)}) async-start(), calls=%async_computation | async-start | bytes 5242880 | tf_op jit(solution)/shard_map/psum | solution.py:95
Sparse Core Ops, SparseCore 0:
  570.4 252.8 all-reduce.4
  826.8 191.1 all-reduce.2
where the time goes:
time: 1030 us
  blocking collectives  496 us (48%)
  waiting for transfers between devices  437 us (42%)
  matrix products  48.7 us (5%)
  local copies, waits for them, and re-layouts  21.4 us (2%)
  between operations  14.2 us (1%)
    pmax x1, blocking collectives, local(): row_top = lax.pmax(local_top, 'ctx')  249 us
    psum x1, blocking collectives, local(): whole_sum = lax.psum(row_sum, 'ctx')  246 us
    psum x1, waiting for transfers between devices, local(): stretch_mass = lax.psum(mass_term, ('ctx', 'head'))  245 us
    psum x1, waiting for transfers between devices, local(): whole_out = lax.psum(scaled, 'ctx')  193 us
    dot_general x24, matrix products, score_block(): jnp.einsum('qgjd,kgd->gjqk', q_block, key_rows, preferred_element_type=jn...  35.8 us
  transfers between devices with their start and end apart: 2, of which 2 were waited for; matrix products, arithmetic and copies ran while one was open for 1% of the time, Pallas kernels for 0%

commit v1 on v0

v1 whole, which is shorter than its diff:
```python
import functools
import math

import jax
import jax.numpy as jnp
import numpy as np
from jax import lax
from jax.experimental import pallas as pl
from jax.experimental.pallas import tpu as pltpu
from jax.sharding import PartitionSpec as P

HD = 128
HALF = HD // 2
ROPE_BASE = 1000000.0
MESH = pl.DeviceIdType.MESH
NX, NY, NZ, NC = 4, 4, 8, 2
NQ = 512
TOK = 512
NCH = 256
HEADS = 10
KV = 2
GROUP = HEADS // KV
ROWS = NQ // (NX * NZ * NC)
LSE_ROWS = 16
HALF_Q = NQ // NC
MASS_ROWS = NCH // (NC * NY * NX)
GW = GROUP * HD


def kernel(
    q_ref, k_ref, v_ref, len_ref, pos_ref, freq_ref, att_ref, mass_ref,
    tab, w_mat, ot, mh, tops, lse, lse_in, lsx, lsx_in, lsz, lsz_in, lsg, lsg_in,
    osum, oc_in, ofar_in, onear_in, oz_in,
    mpart, mc_in, my_in, mx_in, mz, mz_in, mfull,
    s_core, r_core, s_lx, r_lx, s_lz, r_lz, s_ox, r_ox, s_oz, r_oz,
    s_my, r_my, s_mx, r_mx, s_mz, r_mz, s_gx, r_gx, s_gy, r_gy,
):
    ctx = lax.axis_index("ctx")
    y = lax.axis_index("head")
    x = ctx // (NZ * NC)
    z = (ctx // NC) % NZ
    c = ctx % NC
    oc = 1 - c

    def at(xx, zz, cc, yy):
        return ((xx * NZ + zz) * NC + cc, yy)

    partner = at(x, z, oc, y)

    def xpeer(d):
        return at((x + d) % NX, z, c, y)

    def zpeer(d):
        return at(x, (z + d) % NZ, c, y)

    def ypeer(d):
        return at(x, z, c, (y + d) % NY)

    def send(src, dst, ssem, rsem, dev):
        copy = pltpu.make_async_remote_copy(
            src_ref=src, dst_ref=dst, send_sem=ssem, recv_sem=rsem,
            device_id=dev, device_id_type=MESH,
        )
        copy.start()
        return copy

    barrier = pltpu.get_barrier_semaphore()
    peers = [partner] + [xpeer(d) for d in range(1, NX)]
    peers += [zpeer(d) for d in range(1, NZ)] + [ypeer(d) for d in range(1, NY)]
    for dev in peers:
        pl.semaphore_signal(barrier, inc=1, device_id=dev, device_id_type=MESH)

    angles = freq_ref[:, :1] * pos_ref[...].astype(jnp.float32)
    cosine = jnp.cos(angles).T
    sine = jnp.sin(angles).T
    tab[0] = jnp.concatenate([cosine, cosine], axis=1)
    tab[1] = jnp.concatenate([-sine, sine], axis=1)

    lens = len_ref[...].astype(jnp.float32)
    row = lax.broadcasted_iota(jnp.int32, (NCH, NCH), 0)
    col = lax.broadcasted_iota(jnp.int32, (NCH, NCH), 1)
    starts = jnp.sum(jnp.where(col < row, lens, 0.0), axis=1, keepdims=True)
    ends = jnp.sum(jnp.where(col <= row, lens, 0.0), axis=1, keepdims=True)
    token = (lax.broadcasted_iota(jnp.int32, (NCH, TOK), 1) + ctx * TOK).astype(jnp.float32)
    member = jnp.where((token >= starts) & (token < ends), 1.0, 0.0).astype(jnp.bfloat16)
    for g in range(KV):
        w_mat[g, HD:, :] = member
        w_mat[g, :HD, :] = v_ref[:, g * HD : (g + 1) * HD].astype(jnp.float32).T.astype(jnp.bfloat16)

    scale = HD ** -0.5
    exp_scale = scale * math.log2(math.e)
    lse[...] = jnp.zeros_like(lse)
    tops[...] = jnp.zeros_like(tops)

    for g in range(KV):

        def head(j, carry):
            h = g * GROUP + j
            cols = pl.ds(pl.multiple_of(h * HD, HD), HD)
            qh = q_ref[:, cols].astype(jnp.float32)
            roped = (qh * tab[0] + pltpu.roll(qh, HALF, 1) * tab[1]).astype(jnp.bfloat16)
            s = lax.dot_general(
                k_ref[:, g * HD : (g + 1) * HD], roped, (((1,), (1,)), ((), ())),
                preferred_element_type=jnp.float32,
            )
            top = jnp.max(s, axis=0, keepdims=True)
            p = jnp.exp2((s - top) * exp_scale)
            total = jnp.sum(p, axis=0, keepdims=True)
            both = jnp.dot(w_mat[g], p.astype(jnp.bfloat16), preferred_element_type=jnp.float32)
            ot[h] = both[:HD]
            mh[h] = both[HD:]
            tops[pl.ds(h, 1), :] = top * scale
            lse[pl.ds(h, 1), :] = top * scale + jnp.log(total)
            return carry

        lax.fori_loop(0, GROUP, head, 0)

    pl.semaphore_wait(barrier, len(peers))

    def merge(parts):
        top = functools.reduce(jnp.maximum, parts)
        return top + jnp.log(sum(jnp.exp(part - top) for part in parts))

    copy = send(lse, lse_in, s_core.at[0], r_core.at[0], partner)
    copy.wait()
    my_q = pl.ds(pl.multiple_of(c * HALF_Q, HALF_Q), HALF_Q)
    its_q = pl.ds(pl.multiple_of(oc * HALF_Q, HALF_Q), HALF_Q)
    lsx[...] = merge([lse[:, my_q], lse_in[:, my_q]])
    copies = [send(lsx, lsx_in.at[d - 1], s_lx.at[d - 1], r_lx.at[d - 1], xpeer(d)) for d in range(1, NX)]
    for copy in copies:
        copy.wait()
    lsz[...] = merge([lsx[...]] + [lsx_in[d] for d in range(NX - 1)])
    copies = [send(lsz, lsz_in.at[d - 1], s_lz.at[d - 1], r_lz.at[d - 1], zpeer(d)) for d in range(1, NZ)]
    for copy in copies:
        copy.wait()
    lsg[...] = merge([lsz[...]] + [lsz_in[d] for d in range(NZ - 1)])
    copy = send(lsg, lsg_in, s_core.at[1], r_core.at[1], partner)
    copy.wait()
    own_w = jnp.exp(tops[:, my_q] - lsg[...])
    its_w = jnp.exp(tops[:, its_q] - lsg_in[...])
    tops[:, my_q] = own_w
    tops[:, its_q] = its_w

    factor = NCH / (HEADS * NY)
    for cc in range(NC):
        for yy in range(NY):
            base = (cc * NY + yy) * NX * MASS_ROWS
            block = sum(
                mh[h, base : base + NX * MASS_ROWS, :] * tops[h : h + 1, :] for h in range(HEADS)
            )
            mpart[cc, yy] = (block * factor).reshape(NX, MASS_ROWS, NQ)
    m_core = send(mpart.at[oc], mc_in, s_core.at[2], r_core.at[2], partner)

    for h in range(HEADS):
        g, j = h // GROUP, h % GROUP
        turned = (ot[h] * tops[h : h + 1, :]).T.reshape(NX, NZ, NC, ROWS, HD)
        for cc in range(NC):
            osum[cc, g, :, :, :, j * HD : (j + 1) * HD] = turned[:, :, cc]
    o_core = send(osum.at[oc], oc_in, s_core.at[3], r_core.at[3], partner)

    m_core.wait()
    mc_in[...] = mc_in[...] + mpart[c]
    my_copies = [
        send(mc_in.at[(y + d) % NY], my_in.at[d - 1], s_my.at[d - 1], r_my.at[d - 1], ypeer(d))
        for d in range(1, NY)
    ]

    o_core.wait()
    far = (x + 2) % NX
    right = (x + 1) % NX
    left = (x + 3) % NX
    for g in range(KV):
        oc_in[g] = oc_in[g] + osum[c, g]
    ox_copies = [
        send(oc_in.at[0, far], ofar_in.at[0], s_ox.at[0], r_ox.at[0], xpeer(1)),
        send(oc_in.at[1, far], ofar_in.at[1], s_ox.at[1], r_ox.at[1], xpeer(3)),
        send(oc_in.at[1, right], onear_in.at[0, 1], s_ox.at[2], r_ox.at[2], xpeer(1)),
        send(oc_in.at[0, left], onear_in.at[1, 0], s_ox.at[3], r_ox.at[3], xpeer(3)),
    ]

    for copy in my_copies:
        copy.wait()
    mx = mc_in.at[y]
    mx[...] = mc_in[y] + my_in[0] + my_in[1] + my_in[2]
    mx_copies = [
        send(mc_in.at[y, (x + d) % NX], mx_in.at[d - 1], s_mx.at[d - 1], r_mx.at[d - 1], xpeer(d))
        for d in range(1, NX)
    ]

    ox_copies[0].wait()
    oc_in[0, right] = oc_in[0, right] + ofar_in[0]
    ox_copies.append(send(oc_in.at[0, right], onear_in.at[0, 0], s_ox.at[4], r_ox.at[4], xpeer(1)))
    ox_copies[1].wait()
    oc_in[1, left] = oc_in[1, left] + ofar_in[1]
    ox_copies.append(send(oc_in.at[1, left], onear_in.at[1, 1], s_ox.at[5], r_ox.at[5], xpeer(3)))

    for copy in mx_copies:
        copy.wait()
    mz[...] = mc_in[y, x] + mx_in[0] + mx_in[1] + mx_in[2]
    mz_copies = [send(mz, mz_in.at[d - 1], s_mz.at[d - 1], r_mz.at[d - 1], zpeer(d)) for d in range(1, NZ)]

    for copy in ox_copies[2:]:
        copy.wait()
    for g in range(KV):
        oc_in[g, x] = oc_in[g, x] + onear_in[0, g] + onear_in[1, g]
    oz_copies = [
        send(oc_in.at[:, x, (z + d) % NZ], oz_in.at[d - 1], s_oz.at[d - 1], r_oz.at[d - 1], zpeer(d))
        for d in range(1, NZ)
    ]

    for copy in mz_copies:
        copy.wait()
    mfull[c, y, x] = functools.reduce(jnp.add, [mz_in[d] for d in range(NZ - 1)], mz[...])
    gx_copies = [
        send(mfull.at[c, y, x], mfull.at[c, y, x], s_gx.at[d - 1], r_gx.at[d - 1], xpeer(d))
        for d in range(1, NX)
    ]
    for copy in gx_copies:
        copy.wait()
    gy_copies = [
        send(mfull.at[c, y], mfull.at[c, y], s_gy.at[d - 1], r_gy.at[d - 1], ypeer(d))
        for d in range(1, NY)
    ]
    for copy in gy_copies:
        copy.wait()
    m_back = send(mfull.at[c], mfull.at[c], s_core.at[4], r_core.at[4], partner)

    for copy in oz_copies:
        copy.wait()
    for g in range(KV):
        out = functools.reduce(jnp.add, [oz_in[d, g] for d in range(NZ - 1)], oc_in[g, x, z])
        att_ref[:, g * GW : (g + 1) * GW] = out.astype(jnp.bfloat16)
    m_back.wait()
    mass_ref[...] = mfull[...].reshape(NCH, NQ)


def local(queries, keys, values, stretch_lengths, query_pos):
    freq = (ROPE_BASE ** (-(np.arange(HALF, dtype=np.float64) * 2.0 / HD))).astype(np.float32)
    freq = jnp.asarray(np.broadcast_to(freq[:, None], (HALF, HD)))
    f32, bf16 = jnp.float32, jnp.bfloat16
    vmem, dma = pltpu.VMEM, pltpu.SemaphoreType.DMA
    return pl.pallas_call(
        kernel,
        out_shape=(
            jax.ShapeDtypeStruct((ROWS, HEADS * HD), bf16),
            jax.ShapeDtypeStruct((NCH, NQ), f32),
        ),
        in_specs=[pl.BlockSpec(memory_space=pltpu.VMEM)] * 6,
        out_specs=[pl.BlockSpec(memory_space=pltpu.VMEM)] * 2,
        scratch_shapes=[
            vmem((2, NQ, HD), f32),
            vmem((KV, HD + NCH, TOK), bf16),
            vmem((HEADS, HD, NQ), f32),
            vmem((HEADS, NCH, NQ), f32),
            vmem((LSE_ROWS, NQ), f32),
            vmem((LSE_ROWS, NQ), f32),
            vmem((LSE_ROWS, NQ), f32),
            vmem((LSE_ROWS, HALF_Q), f32),
            vmem((NX - 1, LSE_ROWS, HALF_Q), f32),
            vmem((LSE_ROWS, HALF_Q), f32),
            vmem((NZ - 1, LSE_ROWS, HALF_Q), f32),
            vmem((LSE_ROWS, HALF_Q), f32),
            vmem((LSE_ROWS, HALF_Q), f32),
            vmem((NC, KV, NX, NZ, ROWS, GW), f32),
            vmem((KV, NX, NZ, ROWS, GW), f32),
            vmem((2, NZ, ROWS, GW), f32),
            vmem((2, KV, NZ, ROWS, GW), f32),
            vmem((NZ - 1, KV, ROWS, GW), f32),
            vmem((NC, NY, NX, MASS_ROWS, NQ), f32),
            vmem((NY, NX, MASS_ROWS, NQ), f32),
            vmem((NY - 1, NX, MASS_ROWS, NQ), f32),
            vmem((NX - 1, MASS_ROWS, NQ), f32),
            vmem((MASS_ROWS, NQ), f32),
            vmem((NZ - 1, MASS_ROWS, NQ), f32),
            vmem((NC, NY, NX, MASS_ROWS, NQ), f32),
            dma((5,)), dma((5,)),
            dma((NX - 1,)), dma((NX - 1,)),
            dma((NZ - 1,)), dma((NZ - 1,)),
            dma((6,)), dma((6,)),
            dma((NZ - 1,)), dma((NZ - 1,)),
            dma((NY - 1,)), dma((NY - 1,)),
            dma((NX - 1,)), dma((NX - 1,)),
            dma((NZ - 1,)), dma((NZ - 1,)),
            dma((NX - 1,)), dma((NX - 1,)),
            dma((NY - 1,)), dma((NY - 1,)),
        ],
        compiler_params=pltpu.CompilerParams(
            collective_id=0, has_side_effects=True, vmem_limit_bytes=60 * 1024 * 1024
        ),
    )(queries, keys, values, stretch_lengths.reshape(1, NCH), query_pos.reshape(1, NQ), freq)


def solution(mesh):
    placed = (P(None, "head"), P("ctx", "head"), P("ctx", "head"), P(), P())
    return jax.shard_map(
        local, mesh=mesh, in_specs=placed, out_specs=(P("ctx", "head"), P()), check_vma=False
    )
```

time: 1030 us -> 67.6 us (0.07)
  blocking collectives: 496 us -> 0 us
  waiting for transfers between devices: 437 us -> 0 us
  Pallas kernels: 0 us -> 62.2 us
  matrix products: 48.7 us -> 0 us
  local copies, waits for them, and re-layouts: 21.4 us -> 4.55 us
  between operations: 14.2 us -> 0.64 us
    psum x2 -> x0, waiting for transfers between devices: 437 us -> none  [the longest x1 245 us: local(): stretch_mass = lax.psum(mass_term, ('ctx', 'head'))]
    pmax x1 -> x0, blocking collectives: 249 us -> none  [local(): row_top = lax.pmax(local_top, 'ctx')]
    psum x1 -> x0, blocking collectives: 246 us -> none  [local(): whole_sum = lax.psum(row_sum, 'ctx')]
    pallas_call x0 -> x1, Pallas kernels: none -> 62.2 us  [local(): pl.pallas_call(kernel, out_shape=(jax.ShapeDtypeStruct((ROWS, HEADS * HD)...]
    dot_general x48 -> x0, matrix products: 48.7 us -> none  [the longest x24 35.8 us: score_block(): jnp.einsum('qgjd,kgd->gjqk', q_block, key_rows, preferred_element_type=jn...]
  transfers between devices with their start and end apart: 2 -> 0, of which waited for: 2 -> 0; matrix products, arithmetic and copies ran while one was open for 1% -> 0% of each run, Pallas kernels for 0% -> 0%
where the time goes in v1:
time: 67.6 us; the launch traced here: 67.4 us
  Pallas kernels  62.2 us (92%)
  local copies, waits for them, and re-layouts  4.55 us (7%)
    pallas_call x1, Pallas kernels, local(): pl.pallas_call(kernel, out_shape=(jax.ShapeDtypeStruct((ROWS, HEADS * HD)...  62.2 us
    unnamed x2, local copies, waits for them, and re-layouts  3.2 us

profile of v1, /device:TPU:1, one launch (start us, length us, event | category | flops | bytes accessed | tf_op | source)
XLA Modules:
  0.0 67.4 jit_solution(11031995183562008202)
XLA Ops:
  0.6 1.3 %jit_solution_.3.freq_ref = f32[64,128]{1,0:T(8,128)} broadcast(f32[64]{0:T(128)} %constant.2.clone), dimensions={0} | broadcast | bytes 33024 | tf_op jit(solution)
  2.0 62.2 %shard_map.77 = (bf16[8,1280]{1,0:T(8,128)(2,1)}, f32[256,512]{1,0:T(8,128)}) custom-call(bf16[512,1280]{1,0:T(8,128)(2,1)} %q_ref.1, bf16[512,256]{1,0:T(8,128)(2,1)} %k_ref.1, bf16[512,256]{1,0:T(8,128)(2,1)} %v_ref.1, s32[1,256]{1,0:T(1,128)} %bitcast.3, s32[1,512]{1,0:T(1,128)} %bitcast.2, f32[64,128]{1,0:T(8,128)} %jit_solution_.3.freq_ref), custom_call_target="tpu_custom_call" | custom-call | tf_op jit(solution)/shard_map/pallas_call | solution.py:242
  64.2 1.3 %copy.10 = bf16[8,1280]{1,0:T(8,128)(2,1)} copy(bf16[8,1280]{1,0:T(8,128)(2,1)} %get-tuple-element.4) | data formatting | bytes 40960
  65.5 1.9 %copy.11 = f32[256,512]{1,0:T(8,128)} copy(f32[256,512]{1,0:T(8,128)} %get-tuple-element.5) | data formatting | bytes 1048576

commit v2 on v1

v2 whole, which is shorter than its diff:
```python
import functools
import math

import jax
import jax.numpy as jnp
import numpy as np
from jax import lax
from jax.experimental import pallas as pl
from jax.experimental.pallas import tpu as pltpu
from jax.sharding import PartitionSpec as P

HD = 128
HALF = HD // 2
ROPE_BASE = 1000000.0
MESH = pl.DeviceIdType.MESH
NX, NY, NZ, NC = 4, 4, 8, 2
NQ = 512
TOK = 512
NCH = 256
HEADS = 10
KV = 2
GROUP = HEADS // KV
ROWS = NQ // (NX * NZ * NC)
CHIP_ROWS = ROWS * NC
PAD = 8
MASS_ROWS = NCH // (NC * NY * NX)
GW = GROUP * HD
XY = [(dx, dy) for dx in range(NX) for dy in range(NY) if dx or dy]
FREQ = [float(np.float32(ROPE_BASE ** (-2.0 * i / HD))) for i in range(HALF)]


def kernel(
    q_ref, k_ref, v_ref, len_ref, pos_ref, att_ref, mass_ref,
    tab, rp, keys, w_mat, kv_out, kv_in, ot, mh, tops, lse,
    lsx, lsx_in, lsz, lsz_in, osum, ofar_in, onear_in, oz_in, oc_out, oc_in,
    mpart, mc_in, mx_in, mz, mz_in, mfull,
    s_core, r_core, s_lx, r_lx, s_lz, r_lz, s_ox, r_ox, s_oz, r_oz,
    s_mx, r_mx, s_mz, r_mz, s_gx, r_gx,
):
    ctx = lax.axis_index("ctx")
    y = lax.axis_index("head")
    x = ctx // (NZ * NC)
    z = (ctx // NC) % NZ
    c = ctx % NC
    oc = 1 - c

    def at(xx, zz, cc, yy):
        return ((xx * NZ + zz) * NC + cc, yy)

    partner = at(x, z, oc, y)

    def xpeer(d):
        return at((x + d) % NX, z, c, y)

    def zpeer(d):
        return at(x, (z + d) % NZ, c, y)

    def xypeer(dx, dy):
        return at((x + dx) % NX, z, c, (y + dy) % NY)

    def send(src, dst, ssem, rsem, dev):
        copy = pltpu.make_async_remote_copy(
            src_ref=src, dst_ref=dst, send_sem=ssem, recv_sem=rsem,
            device_id=dev, device_id_type=MESH,
        )
        copy.start()
        return copy

    barrier = pltpu.get_barrier_semaphore()
    peers = [partner] + [zpeer(d) for d in range(1, NZ)] + [xypeer(dx, dy) for dx, dy in XY]
    for dev in peers:
        pl.semaphore_signal(barrier, inc=1, device_id=dev, device_id_type=MESH)

    mine = pl.ds(pl.multiple_of(c * HD, HD), HD)
    other = pl.ds(pl.multiple_of(oc * HD, HD), HD)
    kv_out[0] = k_ref[:, other].astype(jnp.float32)
    kv_out[1] = v_ref[:, other].astype(jnp.float32)
    keys[0] = k_ref[:, mine]

    freq_row = lax.broadcasted_iota(jnp.int32, (HALF, HD), 0)
    freq = jnp.zeros((HALF, HD), jnp.float32)
    for i in range(HALF):
        freq = jnp.where(freq_row == i, FREQ[i], freq)
    angles = freq[:, :1] * pos_ref[...].astype(jnp.float32)
    cosine = jnp.cos(angles).T
    sine = jnp.sin(angles).T
    tab[0] = jnp.concatenate([cosine, cosine], axis=1)
    tab[1] = jnp.concatenate([-sine, sine], axis=1)

    lens = len_ref[...].astype(jnp.float32)
    row = lax.broadcasted_iota(jnp.int32, (NCH, NCH), 0)
    col = lax.broadcasted_iota(jnp.int32, (NCH, NCH), 1)
    starts = jnp.sum(jnp.where(col < row, lens, 0.0), axis=1, keepdims=True)
    ends = jnp.sum(jnp.where(col <= row, lens, 0.0), axis=1, keepdims=True)
    for half, shard in enumerate((ctx, ctx - c + oc)):
        token = (lax.broadcasted_iota(jnp.int32, (NCH, TOK), 1) + shard * TOK).astype(jnp.float32)
        member = jnp.where((token >= starts) & (token < ends), 1.0, 0.0).astype(jnp.bfloat16)
        w_mat[half, HD:, :] = member
    w_mat[0, :HD, :] = v_ref[:, mine].astype(jnp.float32).T.astype(jnp.bfloat16)

    scale = HD ** -0.5
    exp_scale = scale * math.log2(math.e)
    lse[...] = jnp.zeros_like(lse)
    tops[...] = jnp.zeros_like(tops)

    def rotate(j):
        cols = pl.ds(pl.multiple_of(c * GW + j * HD, HD), HD)
        qh = q_ref[:, cols].astype(jnp.float32)
        rp[j] = (qh * tab[0] + pltpu.roll(qh, HALF, 1) * tab[1]).astype(jnp.bfloat16)

    def attend(half, j):
        s = lax.dot_general(
            keys[half], rp[j], (((1,), (1,)), ((), ())), preferred_element_type=jnp.float32
        )
        top = jnp.max(s, axis=0, keepdims=True)
        p = jnp.exp2((s - top) * exp_scale)
        total = jnp.sum(p, axis=0, keepdims=True)
        both = jnp.dot(w_mat[half], p.astype(jnp.bfloat16), preferred_element_type=jnp.float32)
        ot[half, j] = both[:HD]
        mh[half, j] = both[HD:]
        tops[half, pl.ds(j, 1), :] = top * scale
        lse[half, pl.ds(j, 1), :] = top * scale + jnp.log(total)

    def first(j, carry):
        rotate(j)
        attend(0, j)
        return carry

    def second(j, carry):
        attend(1, j)
        return carry

    early = 3
    lax.fori_loop(0, early, first, 0)
    pl.semaphore_wait(barrier, len(peers))
    kv_copy = send(kv_out, kv_in, s_core.at[0], r_core.at[0], partner)
    lax.fori_loop(early, GROUP, first, 0)
    kv_copy.wait()
    keys[1] = kv_in[0].astype(jnp.bfloat16)
    w_mat[1, :HD, :] = kv_in[1].T.astype(jnp.bfloat16)
    lax.fori_loop(0, GROUP, second, 0)

    def merge(parts):
        top = functools.reduce(jnp.maximum, parts)
        return top + jnp.log(sum(jnp.exp(part - top) for part in parts))

    lsx[...] = merge([lse[0], lse[1]])
    lx_copies = [send(lsx, lsx_in.at[d - 1], s_lx.at[d - 1], r_lx.at[d - 1], xpeer(d)) for d in range(1, NX)]
    for copy in lx_copies:
        copy.wait()
    lsz[...] = merge([lsx[...]] + [lsx_in[d] for d in range(NX - 1)])
    lz_copies = [send(lsz, lsz_in.at[d - 1], s_lz.at[d - 1], r_lz.at[d - 1], zpeer(d)) for d in range(1, NZ)]

    scales = [jnp.exp(tops[half] - lsz[...]) for half in range(NC)]
    for j in range(GROUP):
        turned = ot[0, j] * scales[0][j : j + 1, :] + ot[1, j] * scales[1][j : j + 1, :]
        osum[:, :, :, j * HD : (j + 1) * HD] = turned.T.reshape(NX, NZ, CHIP_ROWS, HD)
    far = (x + 2) % NX
    right = (x + 1) % NX
    left = (x + 3) % NX
    low, high = pl.ds(0, NZ // 2), pl.ds(NZ // 2, NZ // 2)
    ox_copies = [
        send(osum.at[far, low], ofar_in.at[0], s_ox.at[0], r_ox.at[0], xpeer(1)),
        send(osum.at[far, high], ofar_in.at[1], s_ox.at[1], r_ox.at[1], xpeer(3)),
        send(osum.at[right, high], onear_in.at[0, high], s_ox.at[2], r_ox.at[2], xpeer(1)),
        send(osum.at[left, low], onear_in.at[1, low], s_ox.at[3], r_ox.at[3], xpeer(3)),
    ]

    for copy in lz_copies:
        copy.wait()
    whole = merge([lsz[...]] + [lsz_in[d] for d in range(NZ - 1)])

    factor = NCH / (HEADS * NY)
    weights = [jnp.exp(tops[half] - whole) * factor for half in range(NC)]
    for cc in range(NC):
        for xx in range(NX):
            base = (cc * NX + xx) * NY * MASS_ROWS
            block = sum(
                mh[half, j, base : base + NY * MASS_ROWS, :] * weights[half][j : j + 1, :]
                for half in range(NC)
                for j in range(GROUP)
            )
            mpart[cc, xx] = block.reshape(NY, MASS_ROWS, NQ)
    m_core = send(mpart.at[oc], mc_in, s_core.at[1], r_core.at[1], partner)
    lsz[...] = jnp.exp(lsz[...] - whole)
    m_core.wait()
    mc_in[...] = mc_in[...] + mpart[c]
    mx_copies = [
        send(
            mc_in.at[(x + dx) % NX, (y + dy) % NY], mx_in.at[i], s_mx.at[i], r_mx.at[i],
            xypeer(dx, dy),
        )
        for i, (dx, dy) in enumerate(XY)
    ]

    ox_copies[0].wait()
    osum[right, low] = osum[right, low] + ofar_in[0]
    ox_copies.append(send(osum.at[right, low], onear_in.at[0, low], s_ox.at[4], r_ox.at[4], xpeer(1)))
    ox_copies[1].wait()
    osum[left, high] = osum[left, high] + ofar_in[1]
    ox_copies.append(send(osum.at[left, high], onear_in.at[1, high], s_ox.at[5], r_ox.at[5], xpeer(3)))

    for copy in mx_copies:
        copy.wait()
    mz[...] = functools.reduce(jnp.add, [mx_in[i] for i in range(len(XY))], mc_in[x, y])
    mz_copies = [send(mz, mz_in.at[d - 1], s_mz.at[d - 1], r_mz.at[d - 1], zpeer(d)) for d in range(1, NZ)]

    for copy in ox_copies[2:]:
        copy.wait()
    change = lsz[:, pl.ds(pl.multiple_of(x * HD, HD), HD)].T
    for zz in range(NZ):
        rows = change[zz * CHIP_ROWS : (zz + 1) * CHIP_ROWS]
        for j in range(GROUP):
            cols = slice(j * HD, (j + 1) * HD)
            osum[x, zz, :, cols] = (
                osum[x, zz, :, cols] + onear_in[0, zz, :, cols] + onear_in[1, zz, :, cols]
            ) * rows[:, j : j + 1]
    oz_copies = [
        send(osum.at[x, (z + d) % NZ], oz_in.at[d - 1], s_oz.at[d - 1], r_oz.at[d - 1], zpeer(d))
        for d in range(1, NZ)
    ]

    for copy in mz_copies:
        copy.wait()
    mfull[c, x, y] = functools.reduce(jnp.add, [mz_in[d] for d in range(NZ - 1)], mz[...])
    gx_copies = [
        send(mfull.at[c, x, y], mfull.at[c, x, y], s_gx.at[i], r_gx.at[i], xypeer(dx, dy))
        for i, (dx, dy) in enumerate(XY)
    ]

    for copy in oz_copies:
        copy.wait()
    oc_out[...] = functools.reduce(
        jnp.add, [oz_in[d] for d in range(NZ - 1)], osum[x, z]
    ).reshape(NC, ROWS, GW)
    o_core = send(oc_out.at[oc], oc_in, s_core.at[2], r_core.at[2], partner)

    for copy in gx_copies:
        copy.wait()
    m_back = send(mfull.at[c], mfull.at[c], s_core.at[3], r_core.at[3], partner)
    o_core.wait()
    own, received = oc_out[c], oc_in[...]
    att_ref[:, :GW] = jnp.where(c == 0, own, received).astype(jnp.bfloat16)
    att_ref[:, GW:] = jnp.where(c == 0, received, own).astype(jnp.bfloat16)
    m_back.wait()
    mass_ref[...] = mfull[...].reshape(NCH, NQ)


def local(queries, keys, values, stretch_lengths, query_pos):
    f32, bf16 = jnp.float32, jnp.bfloat16
    vmem, dma = pltpu.VMEM, pltpu.SemaphoreType.DMA
    return pl.pallas_call(
        kernel,
        out_shape=(
            jax.ShapeDtypeStruct((ROWS, HEADS * HD), bf16),
            jax.ShapeDtypeStruct((NCH, NQ), f32),
        ),
        in_specs=[pl.BlockSpec(memory_space=pltpu.VMEM)] * 5,
        out_specs=[pl.BlockSpec(memory_space=pltpu.VMEM)] * 2,
        scratch_shapes=[
            vmem((2, NQ, HD), f32),
            vmem((GROUP, NQ, HD), bf16),
            vmem((NC, TOK, HD), bf16),
            vmem((NC, HD + NCH, TOK), bf16),
            vmem((2, TOK, HD), f32),
            vmem((2, TOK, HD), f32),
            vmem((NC, GROUP, HD, NQ), f32),
            vmem((NC, GROUP, NCH, NQ), f32),
            vmem((NC, PAD, NQ), f32),
            vmem((NC, PAD, NQ), f32),
            vmem((PAD, NQ), f32),
            vmem((NX - 1, PAD, NQ), f32),
            vmem((PAD, NQ), f32),
            vmem((NZ - 1, PAD, NQ), f32),
            vmem((NX, NZ, CHIP_ROWS, GW), f32),
            vmem((2, NZ // 2, CHIP_ROWS, GW), f32),
            vmem((2, NZ, CHIP_ROWS, GW), f32),
            vmem((NZ - 1, CHIP_ROWS, GW), f32),
            vmem((NC, ROWS, GW), f32),
            vmem((ROWS, GW), f32),
            vmem((NC, NX, NY, MASS_ROWS, NQ), f32),
            vmem((NX, NY, MASS_ROWS, NQ), f32),
            vmem((len(XY), MASS_ROWS, NQ), f32),
            vmem((MASS_ROWS, NQ), f32),
            vmem((NZ - 1, MASS_ROWS, NQ), f32),
            vmem((NC, NX, NY, MASS_ROWS, NQ), f32),
            dma((4,)), dma((4,)),
            dma((NX - 1,)), dma((NX - 1,)),
            dma((NZ - 1,)), dma((NZ - 1,)),
            dma((6,)), dma((6,)),
            dma((NZ - 1,)), dma((NZ - 1,)),
            dma((len(XY),)), dma((len(XY),)),
            dma((NZ - 1,)), dma((NZ - 1,)),
            dma((len(XY),)), dma((len(XY),)),
        ],
        compiler_params=pltpu.CompilerParams(
            collective_id=0, has_side_effects=True, vmem_limit_bytes=60 * 1024 * 1024
        ),
    )(queries, keys, values, stretch_lengths.reshape(1, NCH), query_pos.reshape(1, NQ))


def solution(mesh):
    placed = (P(None, "head"), P("ctx", "head"), P("ctx", "head"), P(), P())
    return jax.shard_map(
        local, mesh=mesh, in_specs=placed, out_specs=(P("ctx", "head"), P()), check_vma=False
    )
```

time: 67.6 us -> 57 us (0.84)
  Pallas kernels: 62.2 us -> 52.3 us
  local copies, waits for them, and re-layouts: 4.55 us -> 3.2 us
    pallas_call x1, Pallas kernels: 62.2 us -> 52.3 us  [local(): pl.pallas_call(kernel, out_shape=(jax.ShapeDtypeStruct((ROWS, HEADS * HD)...]
    another operation x1 -> x0, local copies, waits for them, and re-layouts: 1.35 us -> none
where the time goes in v2:
time: 57 us; the launch traced here: 56.1 us
  Pallas kernels  52.3 us (92%)
  local copies, waits for them, and re-layouts  3.2 us (6%)
  between operations  0.64 us (1%)
    pallas_call x1, Pallas kernels, local(): pl.pallas_call(kernel, out_shape=(jax.ShapeDtypeStruct((ROWS, HEADS * HD)...  52.3 us
    unnamed x2, local copies, waits for them, and re-layouts  3.2 us

profile of v2, /device:TPU:1, one launch (start us, length us, event | category | flops | bytes accessed | tf_op | source)
XLA Modules:
  0.0 56.1 jit_solution(8488940705251143243)
XLA Ops:
  0.6 52.3 %shard_map.68 = (bf16[8,1280]{1,0:T(8,128)(2,1)}, f32[256,512]{1,0:T(8,128)}) custom-call(bf16[512,1280]{1,0:T(8,128)(2,1)} %q_ref.1, bf16[512,256]{1,0:T(8,128)(2,1)} %k_ref.1, bf16[512,256]{1,0:T(8,128)(2,1)} %v_ref.1, s32[1,256]{1,0:T(1,128)} %bitcast.3, s32[1,512]{1,0:T(1,128)} %bitcast.2), custom_call_target="tpu_custom_call" | custom-call | tf_op jit(solution)/shard_map/pallas_call | solution.py:252
  52.9 1.3 %copy.9 = bf16[8,1280]{1,0:T(8,128)(2,1)} copy(bf16[8,1280]{1,0:T(8,128)(2,1)} %get-tuple-element.4) | data formatting | bytes 40960
  54.3 1.9 %copy.10 = f32[256,512]{1,0:T(8,128)} copy(f32[256,512]{1,0:T(8,128)} %get-tuple-element.5) | data formatting | bytes 1048576
